TPU v7x, 32 devices: a whole 2x2x4 slice. The times are simulated.
32 devices in a mesh: rows: 4 (over z), chan: 8 (over y, x, core).
Axes of the slice: x: 2, y: 2, z: 4, core: 2. Of those that a mesh axis runs over, the one named last changes fastest.
Arguments:
- feats: bfloat16 [64, 1024, 1024], P('rows', 'chan'), may hold values from -140 to 140
- norm_gain: float32 [1024], P('chan'), may hold values from 0.1 to 1.9
- proj_weight: float32 [8, 1024], P(None, 'chan'), may hold values from -320 to 320
- chan_bias: float32 [1024], P('chan'), may hold values from -8 to -2
Outputs:
- mixed: bfloat16 [64, 1024, 1024], P('rows', 'chan')
All inputs are finite; a program needn't handle non-finite values.
Results may differ from a plain program's by a relative error of at most 0.001.
Values sent between devices are 32-bit elements; how exact they have to be, the bound alone decides.
A program may use at most 128 MiB of HBM per device.

v0:
```python
import jax
import jax.numpy as jnp
from jax import lax
from jax.sharding import PartitionSpec as P

CHANNELS = 1024
EPSILON = 1e-05


def advance(current, row_weights, row_rate):
    edge_zero = jnp.zeros_like(current[:, :1])
    left_side = jnp.concatenate([edge_zero, current[:, :-1]], axis=1)
    right_side = jnp.concatenate([current[:, 1:], edge_zero], axis=1)
    blended = (
        row_weights[0][None, :] * left_side
        + row_weights[1][None, :] * current
        + row_weights[2][None, :] * right_side
    )
    return (1.0 - row_rate) * blended


def coefficients(logits, chan_bias, offset):
    weights = jax.nn.softmax(logits[:, offset : offset + 3, :], axis=1)
    rates = jax.nn.sigmoid(logits[:, 6 + offset // 3, :][:, None, :] + chan_bias[None, :, None])
    return (weights, rates)


def sweep_rows(start, weights, rates, drive, reverse, keep):

    def sweep_row_step(current, inputs):
        row_weights, row_rate, row_drive = inputs
        current = advance(current, row_weights, row_rate) + row_drive
        return (current, current if keep else None)

    return lax.scan(sweep_row_step, start, (weights, rates, drive), reverse=reverse)


def carry_through(start, weights, rates, reverse):

    def carry_row_step(current, inputs):
        return (advance(current, inputs[0], inputs[1]), None)

    finished, _ = lax.scan(carry_row_step, start, (weights, rates), reverse=reverse)
    return finished


def shards(feats, norm_gain, proj_weight, chan_bias):
    logit_scale = CHANNELS ** (-0.5)
    values = feats.astype(jnp.float32)
    squares = jnp.sum(values * values, axis=1)
    square_total = lax.psum(squares, "chan")
    inverse = 1.0 / jnp.sqrt(square_total / CHANNELS + EPSILON)
    normed = values * inverse[:, None, :] * norm_gain[None, :, None]
    projected = jnp.einsum(
        "jc,rcw->rjw",
        proj_weight,
        normed,
        precision=lax.Precision.HIGHEST,
        preferred_element_type=jnp.float32,
    )
    logits = lax.psum(projected, "chan") * logit_scale
    down_weights, down_rate = coefficients(logits, chan_bias, 0)
    up_weights, up_rate = coefficients(logits, chan_bias, 3)
    down_drive = jnp.sqrt(down_rate) * normed
    up_drive = jnp.sqrt(up_rate) * normed
    anchor = jnp.zeros((feats.shape[1], feats.shape[2]), jnp.float32)
    down_local, _ = sweep_rows(anchor, down_weights, down_rate, down_drive, False, False)
    up_local, _ = sweep_rows(anchor, up_weights, up_rate, up_drive, True, False)
    gathered, down_ends, up_ends = (
        lax.all_gather(logits, "rows", axis=0, tiled=True),
        lax.all_gather(down_local, "rows", axis=0, tiled=True),
        lax.all_gather(up_local, "rows", axis=0, tiled=True),
    )
    position = lax.axis_index("rows")
    devices = lax.axis_size("rows")
    block_rows = logits.shape[0]
    local_chans = feats.shape[1]

    def down_visit(visited, current):
        visited = jnp.asarray(visited).astype(jnp.int32)
        block_logits = lax.dynamic_slice_in_dim(gathered, visited * block_rows, block_rows, 0)
        block_weights, block_rates = coefficients(block_logits, chan_bias, 0)
        block_end = lax.dynamic_slice_in_dim(down_ends, visited * local_chans, local_chans, 0)
        return carry_through(current, block_weights, block_rates, False) + block_end

    def up_visit(turn, current):
        visited = (devices - 1 - jnp.asarray(turn)).astype(jnp.int32)
        block_logits = lax.dynamic_slice_in_dim(gathered, visited * block_rows, block_rows, 0)
        block_weights, block_rates = coefficients(block_logits, chan_bias, 3)
        block_end = lax.dynamic_slice_in_dim(up_ends, visited * local_chans, local_chans, 0)
        return carry_through(current, block_weights, block_rates, True) + block_end

    down_in = lax.fori_loop(0, position, down_visit, anchor)
    up_in = lax.fori_loop(0, devices - 1 - position, up_visit, anchor)
    _, down_rows = sweep_rows(down_in, down_weights, down_rate, down_drive, False, True)
    _, up_rows = sweep_rows(up_in, up_weights, up_rate, up_drive, True, True)
    return (down_rows * up_rows).astype(jnp.bfloat16)


def solution(mesh):
    in_specs = (P("rows", "chan", None), P("chan"), P(None, "chan"), P("chan"))
    out_specs = P("rows", "chan", None)
    return jax.shard_map(shards, mesh=mesh, in_specs=in_specs, out_specs=out_specs, check_vma=False)
```

profile of v0, /device:TPU:0, one launch (start us, length us, event | category | flops | bytes accessed | tf_op | source)
XLA Modules:
  0.0 489.4 jit_solution(14477030094933963573)
XLA Ops:
  6.5 3.9 fusion.28
  10.5 56.0 %all-reduce.15.cloned.1.call-done = f32[16,1024]{1,0:T(8,128)} async-done(((f32[16,1024]{1,0:T(8,128)}), f32[16,1024]{1,0:T(8,128)}) %all-reduce.15.cloned.1.call-update) | async-done | bytes 65552 | tf_op jit(solution)/shard_map/psum | solution.py:51
  67.4 7.7 %fusion.36 = f32[16,8,1024]{2,1,0:T(8,128)} fusion(bf16[16,128,1024]{2,1,0:T(8,128)(2,1)} %param.20, f32[128]{0:T(128)} %param.21, f32[16,1024]{1,0:T(8,128)S(1)} %add_rsqrt_fusion, f32[8,128]{1,0:T(8,128)S(1)} %copy-done), kind=kOutput, calls=%fused_computation.76 | convolution fusion | flops 207618048 | bytes 4788736 | tf_op jit(solution)/shard_map/jc,rcw->rjw/dot_general | solution.py:54
  75.1 54.3 %all-reduce.17.cloned.1.call-done = f32[16,8,1024]{2,1,0:T(8,128)} async-done(((f32[16,8,1024]{2,1,0:T(8,128)}), f32[16,8,1024]{2,1,0:T(8,128)}) %all-reduce.17.cloned.1.call-update) | async-done | bytes 524304 | tf_op jit(solution)/shard_map/psum | solution.py:61
  131.1 15.1 %fusion.30 = (f32[16,128,1024]{2,1,0:T(8,128)}, f32[16,128,1024]{2,1,0:T(8,128)}, f32[16,128,1024]{2,1,0:T(8,128)}, f32[16,128,1024]{2,1,0:T(8,128)}) fusion(bf16[16,128,1024]{2,1,0:T(8,128)(2,1)} %param.20, f32[128]{0:T(128)S(1)} %copy-done.6, f32[16,1024]{1,0:T(8,128)S(1)} %add_rsqrt_fusion, f32[128]{0:T(128)S(1)} %copy-done.5, ...), kind=kLoop, calls=%fused_computation.68 | loop fusion | flops 27262976 | bytes 37946368 | tf_op jit(solution)/shard_map/mul | solution.py:65
  146.2 30.4 %while.121 = (s32[]{:T(128)}, f32[128,1024]{1,0:T(8,128)S(1)}, f32[16,128,1024]{2,1,0:T(8,128)}, f32[16,3,1024]{2,1,0:T(4,128)S(1)}, f32[16,128,1024]{2,1,0:T(8,...) while((s32[]{:T(128)}, f32[128,1024]{1,0:T(8,128)S(1)}, ...), condition=%wide.region_18.19_spmd.clone, body=%wide.region_17.18_spmd.clone.sunk | while | flops 1310726 | bytes 6325412 | solution.py:35
  178.1 31.0 %while.120 = (s32[]{:T(128)}, f32[128,1024]{1,0:T(8,128)S(1)}, f32[16,128,1024]{2,1,0:T(8,128)}, f32[16,3,1024]{2,1,0:T(4,128)S(1)}, f32[16,128,1024]{2,1,0:T(8,128)}, /*index=5*/s32[]{:T(128)}, s32[]{:T(128)}, s32[]{}, s32[]{}) while((s32[]{:T(128)}, f32[128,1024]{1,0:T(8,128)S(1)}, f32[16,128,1024]{2,1,0:T(8,128)}, ...), condition=%wide.region_6.0_spmd.clone, body=%wide.region_5.0_spmd.clone.sunk | while | flops 1310725 | bytes 6325392 | solution.py:35
  209.9 12.7 %all-gather.8.cloned.1.call-done = f32[512,1024]{1,0:T(8,128)} async-done(((f32[128,1024]{1,0:T(8,128)}), f32[512,1024]{1,0:T(8,128)}) %all-gather.8.cloned.1.call-update) | async-done | bytes 2097168 | tf_op jit(solution)/shard_map/all_gather | solution.py:72
  222.6 45.9 %all-gather.4.cloned.1.call-done = f32[64,8,1024]{2,1,0:T(8,128)} async-done(((f32[16,8,1024]{2,1,0:T(8,128)}), f32[64,8,1024]{2,1,0:T(8,128)}) %all-gather.4.cloned.1.call-update) | async-done | bytes 2097168 | tf_op jit(solution)/shard_map/all_gather | solution.py:70
  268.6 112.8 %while.118 = (s32[]{:T(128)}, f32[128,1024]{1,0:T(8,128)S(1)}, s32[]{:T(128)}, f32[64,8,1024]{2,1,0:T(8,128)}, f32[128]{0:T(128)S(1)}, /*index=5*/f32[512,1024]{...) while((s32[]{:T(128)}, f32[128,1024]{1,0:T(8,128)S(1)}, ...), condition=%wide.region_24.25_spmd, body=%wide.region_19.24_spmd.sunk | while | flops 9568278 | bytes 15501354 | solution.py:94
  269.9 5.4 %add_divide_fusion.7 = f32[16,128,1024]{2,1,0:T(8,128)} fusion(f32[128]{0:T(128)S(1)} %get-tuple-element.1319, f32[16,1024]{1,0:T(8,128)S(1)} %bitcast.131), kind=kLoop, calls=%fused_computation.30.clone.1 | loop fusion | flops 8388608 | bytes 8454656 | tf_op jit(solution)/shard_map/while/body/div | solution.py:24
  276.8 28.4 %while.123 = (s32[]{:T(128)}, f32[128,1024]{1,0:T(8,128)S(1)}, f32[16,128,1024]{2,1,0:T(8,128)}, f32[16,3,1024]{2,1,0:T(4,128)S(1)}, s32[]{:T(128)}, /*index=5*/s32[]{:T(128)}, s32[]{:T(128)}, s32[]{}, s32[]{}) while((s32[]{:T(128)}, f32[128,1024]{1,0:T(8,128)S(1)}, f32[16,128,1024]{2,1,0:T(8,128)}, f32[16,3,1024]{2,1,0:T(4,128)S(1)}, ...), condition=%wide.region_23.23_spmd, body=%wide.region_22.22_spmd.sunk | while | flops 917509 | bytes 4752529 | solution.py:43
  307.5 5.4 %add_divide_fusion.7 = f32[16,128,1024]{2,1,0:T(8,128)} fusion(f32[128]{0:T(128)S(1)} %get-tuple-element.1319, f32[16,1024]{1,0:T(8,128)S(1)} %bitcast.131), kind=kLoop, calls=%fused_computation.30.clone.1 | loop fusion | flops 8388608 | bytes 8454656 | tf_op jit(solution)/shard_map/while/body/div | solution.py:24
  314.4 28.3 %while.123 = (s32[]{:T(128)}, f32[128,1024]{1,0:T(8,128)S(1)}, f32[16,128,1024]{2,1,0:T(8,128)}, f32[16,3,1024]{2,1,0:T(4,128)S(1)}, s32[]{:T(128)}, /*index=5*/s32[]{:T(128)}, s32[]{:T(128)}, s32[]{}, s32[]{}) while((s32[]{:T(128)}, f32[128,1024]{1,0:T(8,128)S(1)}, f32[16,128,1024]{2,1,0:T(8,128)}, f32[16,3,1024]{2,1,0:T(4,128)S(1)}, ...), condition=%wide.region_23.23_spmd, body=%wide.region_22.22_spmd.sunk | while | flops 917509 | bytes 4752529 | solution.py:43
  345.0 5.4 %add_divide_fusion.7 = f32[16,128,1024]{2,1,0:T(8,128)} fusion(f32[128]{0:T(128)S(1)} %get-tuple-element.1319, f32[16,1024]{1,0:T(8,128)S(1)} %bitcast.131), kind=kLoop, calls=%fused_computation.30.clone.1 | loop fusion | flops 8388608 | bytes 8454656 | tf_op jit(solution)/shard_map/while/body/div | solution.py:24
  351.9 28.3 %while.123 = (s32[]{:T(128)}, f32[128,1024]{1,0:T(8,128)S(1)}, f32[16,128,1024]{2,1,0:T(8,128)}, f32[16,3,1024]{2,1,0:T(4,128)S(1)}, s32[]{:T(128)}, /*index=5*/s32[]{:T(128)}, s32[]{:T(128)}, s32[]{}, s32[]{}) while((s32[]{:T(128)}, f32[128,1024]{1,0:T(8,128)S(1)}, f32[16,128,1024]{2,1,0:T(8,128)}, f32[16,3,1024]{2,1,0:T(4,128)S(1)}, ...), condition=%wide.region_23.23_spmd, body=%wide.region_22.22_spmd.sunk | while | flops 917509 | bytes 4752529 | solution.py:43
  381.4 4.3 broadcast.113.clone.1
  385.6 41.8 %while.119 = (s32[]{:T(128)}, f32[128,1024]{1,0:T(8,128)S(1)}, f32[16,128,1024]{2,1,0:T(8,128)}, f32[16,128,1024]{2,1,0:T(8,128)}, f32[16,3,1024]{2,1,0:T(4,128)...) while((s32[]{:T(128)}, f32[128,1024]{1,0:T(8,128)S(1)}, ...), condition=%wide.region_26.27_spmd, body=%wide.region_25.26_spmd.sunk | while | flops 1048581 | bytes 5801121 | solution.py:35
  385.9 2.4 bitcast_dynamic-update-slice_fusion.5
  393.7 2.4 bitcast_dynamic-update-slice_fusion.5
  401.5 2.4 bitcast_dynamic-update-slice_fusion.5
  409.4 2.4 bitcast_dynamic-update-slice_fusion.5
  414.6 2.4 bitcast_dynamic-update-slice_fusion.5
  419.8 2.4 bitcast_dynamic-update-slice_fusion.5
  422.4 2.4 bitcast_dynamic-update-slice_fusion.5
  427.5 4.3 broadcast.113.clone
  431.8 41.8 %while.116 = (s32[]{:T(128)}, f32[128,1024]{1,0:T(8,128)S(1)}, f32[16,128,1024]{2,1,0:T(8,128)}, f32[16,128,1024]{2,1,0:T(8,128)}, f32[16,3,1024]{2,1,0:T(4,128)...) while((s32[]{:T(128)}, f32[128,1024]{1,0:T(8,128)S(1)}, ...), condition=%wide.region_14.15_spmd, body=%wide.region_13.14_spmd.sunk | while | flops 1048580 | bytes 5801609 | solution.py:35
  437.2 2.4 bitcast_dynamic-update-slice_fusion.4
  458.1 2.4 bitcast_dynamic-update-slice_fusion.4
  460.8 2.4 bitcast_dynamic-update-slice_fusion.4
  471.2 2.4 bitcast_dynamic-update-slice_fusion.4
  473.6 9.3 %multiply_convert_fusion = bf16[16,128,1024]{2,1,0:T(8,128)(2,1)} fusion(f32[16,128,1024]{2,1,0:T(8,128)} %get-tuple-element.568, f32[16,128,1024]{2,1,0:T(8,128)} %get-tuple-element.571), kind=kLoop, calls=%fused_computation.71 | loop fusion | flops 4194304 | bytes 20971520 | tf_op jit(solution)/shard_map/convert_element_type | solution.py:97
  (405 shorter events, 216.8 us)
Async XLA Ops:
  6.5 60.8 %copy-start = (f32[8,128]{1,0:T(8,128)S(1)}, f32[8,128]{1,0:T(8,128)}, u32[]{:S(2)}) copy-start(f32[8,128]{1,0:T(8,128)} %param.22) | copy-start | bytes 12292
  6.5 124.5 %copy-start.6 = (f32[128]{0:T(128)S(1)}, f32[128]{0:T(128)}, u32[]{:S(2)}) copy-start(f32[128]{0:T(128)} %param.21) | copy-start | bytes 1540
  6.5 124.6 %copy-start.5 = (f32[128]{0:T(128)S(1)}, f32[128]{0:T(128)}, u32[]{:S(2)}) copy-start(f32[128]{0:T(128)} %param.23) | copy-start | bytes 1540
  6.5 60.0 %all-reduce.15.cloned.1.call-start = ((), (), s32[]{:S(2)}) async-start(), calls=%async_computation | async-start | bytes 131072 | tf_op jit(solution)/shard_map/psum | solution.py:51
  10.5 119.0 %all-reduce.17.cloned.1.call-start = ((), (), s32[]{:S(2)}) async-start(), calls=%async_computation.1 | async-start | bytes 1048576 | tf_op jit(solution)/shard_map/psum | solution.py:61
  75.1 147.5 %all-gather.8.cloned.1.call-start = ((), (), s32[]{:S(2)}) async-start(), calls=%async_computation.4 | async-start | bytes 2621440 | tf_op jit(solution)/shard_map/all_gather | solution.py:72
  130.5 47.0 %copy-start.4 = (f32[16,8,1024]{2,1,0:T(8,128)}, f32[16,8,1024]{2,1,0:T(8,128)S(1)}, u32[]{:S(2)}) copy-start(f32[16,8,1024]{2,1,0:T(8,128)S(1)} %broadcast_multiply_fusion) | copy-start | bytes 1572868
  176.7 0.8 copy-start.2
  177.5 91.0 %all-gather.4.cloned.1.call-start = ((), (), s32[]{:S(2)}) async-start(), calls=%async_computation.2 | async-start | bytes 2621440 | tf_op jit(solution)/shard_map/all_gather | solution.py:70
  178.1 249.4 %all-gather.6.cloned.1.call-start = ((), (), s32[]{:S(2)}) async-start(), calls=%async_computation.3 | async-start | bytes 2621440 | tf_op jit(solution)/shard_map/all_gather | solution.py:71
  209.1 0.8 copy-start.3
  473.6 9.3 %copy-start.1 = (f32[8,128]{1,0:T(8,128)S(1)}, f32[8,128]{1,0:T(8,128)}, u32[]{:S(2)}) copy-start(f32[8,128]{1,0:T(8,128)} %param.22) | copy-start | bytes 12292
Sparse Core Ops, SparseCore 0:
  10.6 55.8 all-reduce.14
  75.2 54.1 all-reduce.16
  177.6 44.9 all-gather.7
  224.0 44.4 all-gather.3
  269.9 44.4 all-gather.5
where the time goes:
time: 494 us; the launch traced here: 489 us
  other arithmetic  258 us (52%)
  waiting for transfers between devices  169 us (34%)
  local copies, waits for them, and re-layouts  38.3 us (8%)
  between operations  13.3 us (3%)
  matrix products  7.69 us (2%)
    dynamic_update_slice x32, other arithmetic, sweep_rows(): lax.scan(sweep_row_step, start, (weights, rates, drive), reverse=reverse)  76.6 us
    mul x48, other arithmetic, advance(): return (1.0 - row_rate) * blended  73.1 us
    psum x1, waiting for transfers between devices, shards(): square_total = lax.psum(squares, 'chan')  56 us
    psum x1, waiting for transfers between devices, shards(): logits = lax.psum(projected, 'chan') * logit_scale  54.3 us
    add x32, other arithmetic, sweep_row_step(): current = advance(current, row_weights, row_rate) + row_drive  51.8 us
    all_gather x1, waiting for transfers between devices, shards(): lax.all_gather(logits, 'rows', axis=0, tiled=True)  45.9 us
    slice x112, local copies, waits for them, and re-layouts, advance(): left_side = jnp.concatenate([edge_zero, current[:, :-1]], axis=1)  22.6 us
    div x3, other arithmetic, coefficients(): jax.nn.sigmoid(logits[:, 6 + offset // 3, :][:, None, :] + chan_bias[None...  16.3 us
  transfers between devices with their start and end apart: 5, of which 4 were waited for; matrix products, arithmetic and copies ran while one was open for 38% of the time, Pallas kernels for 0%

commit v1 on v0

--- a/solution.py
+++ b/solution.py
@@ -45,10 +45,22 @@
 
 
 def shards(feats, norm_gain, proj_weight, chan_bias):
+
+    def skins_begin(sheet):
+        across = "chan"
+        dev_count = lax.axis_size(across)
+        oldest = sheet
+        for d in [
+            [(i, i ^ at) for i in range(dev_count)] for at in (1, 2, 4, 8, 16) if at < dev_count
+        ]:
+            all_values = lax.ppermute(oldest, across, d)
+            oldest = oldest + all_values
+        return oldest
+
     logit_scale = CHANNELS ** (-0.5)
     values = feats.astype(jnp.float32)
     squares = jnp.sum(values * values, axis=1)
-    square_total = lax.psum(squares, "chan")
+    square_total = skins_begin(squares)
     inverse = 1.0 / jnp.sqrt(square_total / CHANNELS + EPSILON)
     normed = values * inverse[:, None, :] * norm_gain[None, :, None]
     projected = jnp.einsum(

time: 494 us -> 450 us (0.911)
  waiting for transfers between devices: 169 us -> 121 us
  starting transfers between devices: 0.17 us -> 5.52 us
    psum x1 -> x0, waiting for transfers between devices: 56 us -> none  [shards(): square_total = lax.psum(squares, 'chan')]
    ppermute x0 -> x3, waiting for transfers between devices: none -> 5.7 us  [skins_begin(): all_values = lax.ppermute(oldest, across, d)]
    ppermute x0 -> x3, starting transfers between devices: none -> 5.39 us  [skins_begin(): all_values = lax.ppermute(oldest, across, d)]
  transfers between devices with their start and end apart: 5 -> 7, of which waited for: 4 -> 6; matrix products, arithmetic and copies ran while one was open for 38% -> 42% of each run, Pallas kernels for 0% -> 0%
where the time goes in v1:
time: 450 us; the launch traced here: 446 us
  other arithmetic  256 us (57%)
  waiting for transfers between devices  121 us (27%)
  local copies, waits for them, and re-layouts  38.3 us (9%)
  between operations  13.3 us (3%)
  matrix products  7.69 us (2%)
  starting transfers between devices  5.52 us (1%)
    dynamic_update_slice x32, other arithmetic, sweep_rows(): lax.scan(sweep_row_step, start, (weights, rates, drive), reverse=reverse)  76.6 us
    mul x48, other arithmetic, advance(): return (1.0 - row_rate) * blended  73.1 us
    psum x1, waiting for transfers between devices, shards(): logits = lax.psum(projected, 'chan') * logit_scale  56.5 us
    add x32, other arithmetic, sweep_row_step(): current = advance(current, row_weights, row_rate) + row_drive  51.8 us
    all_gather x1, waiting for transfers between devices, shards(): lax.all_gather(logits, 'rows', axis=0, tiled=True)  46.1 us
    slice x112, local copies, waits for them, and re-layouts, advance(): left_side = jnp.concatenate([edge_zero, current[:, :-1]], axis=1)  22.6 us
    div x3, other arithmetic, coefficients(): jax.nn.sigmoid(logits[:, 6 + offset // 3, :][:, None, :] + chan_bias[None...  16.4 us
    mul x1, other arithmetic, shards(): up_drive = jnp.sqrt(up_rate) * normed  15.2 us
  transfers between devices with their start and end apart: 7, of which 6 were waited for; matrix products, arithmetic and copies ran while one was open for 42% of the time, Pallas kernels for 0%

profile of v1, /device:TPU:0, one launch (start us, length us, event | category | flops | bytes accessed | tf_op | source)
XLA Modules:
  0.0 445.5 jit_solution(16679190661572288843)
XLA Ops:
  6.5 3.3 fusion.28
  11.3 2.9 collective-permute-start.1
  14.2 2.4 collective-permute-done.1
  21.0 7.7 %fusion.36 = f32[16,8,1024]{2,1,0:T(8,128)} fusion(bf16[16,128,1024]{2,1,0:T(8,128)(2,1)} %param.20, f32[128]{0:T(128)} %param.21, f32[16,1024]{1,0:T(8,128)S(1)} %add_rsqrt_fusion, f32[8,128]{1,0:T(8,128)S(1)} %copy-done), kind=kOutput, calls=%fused_computation.76 | convolution fusion | flops 207618048 | bytes 4788736 | tf_op jit(solution)/shard_map/jc,rcw->rjw/dot_general | solution.py:66
  28.7 56.5 %all-reduce.14.cloned.1.call-done = f32[16,8,1024]{2,1,0:T(8,128)} async-done(((f32[16,8,1024]{2,1,0:T(8,128)}), f32[16,8,1024]{2,1,0:T(8,128)}) %all-reduce.14.cloned.1.call-update) | async-done | bytes 524304 | tf_op jit(solution)/shard_map/psum | solution.py:73
  86.9 15.2 %fusion.30 = (f32[16,128,1024]{2,1,0:T(8,128)}, f32[16,128,1024]{2,1,0:T(8,128)}, f32[16,128,1024]{2,1,0:T(8,128)}, f32[16,128,1024]{2,1,0:T(8,128)}) fusion(bf16[16,128,1024]{2,1,0:T(8,128)(2,1)} %param.20, f32[128]{0:T(128)S(1)} %copy-done.6, f32[16,1024]{1,0:T(8,128)S(1)} %add_rsqrt_fusion, f32[128]{0:T(128)S(1)} %copy-done.5, ...), kind=kLoop, calls=%fused_computation.68 | loop fusion | flops 27262976 | bytes 37946368 | tf_op jit(solution)/shard_map/mul | solution.py:77
  102.1 30.4 %while.121 = (s32[]{:T(128)}, f32[128,1024]{1,0:T(8,128)S(1)}, f32[16,128,1024]{2,1,0:T(8,128)}, f32[16,3,1024]{2,1,0:T(4,128)S(1)}, f32[16,128,1024]{2,1,0:T(8,...) while((s32[]{:T(128)}, f32[128,1024]{1,0:T(8,128)S(1)}, ...), condition=%wide.region_17.18_spmd.clone, body=%wide.region_16.17_spmd.clone.sunk | while | flops 1310726 | bytes 6325412 | solution.py:35
  134.1 31.0 %while.120 = (s32[]{:T(128)}, f32[128,1024]{1,0:T(8,128)S(1)}, f32[16,128,1024]{2,1,0:T(8,128)}, f32[16,3,1024]{2,1,0:T(4,128)S(1)}, f32[16,128,1024]{2,1,0:T(8,128)}, /*index=5*/s32[]{:T(128)}, s32[]{:T(128)}, s32[]{}, s32[]{}) while((s32[]{:T(128)}, f32[128,1024]{1,0:T(8,128)S(1)}, f32[16,128,1024]{2,1,0:T(8,128)}, ...), condition=%wide.region_5.0_spmd.clone, body=%wide.region_4.0_spmd.clone.sunk | while | flops 1310725 | bytes 6325392 | solution.py:35
  165.9 12.5 %all-gather.8.cloned.1.call-done = f32[512,1024]{1,0:T(8,128)} async-done(((f32[128,1024]{1,0:T(8,128)}), f32[512,1024]{1,0:T(8,128)}) %all-gather.8.cloned.1.call-update) | async-done | bytes 2097168 | tf_op jit(solution)/shard_map/all_gather | solution.py:84
  178.4 46.1 %all-gather.4.cloned.1.call-done = f32[64,8,1024]{2,1,0:T(8,128)} async-done(((f32[16,8,1024]{2,1,0:T(8,128)}), f32[64,8,1024]{2,1,0:T(8,128)}) %all-gather.4.cloned.1.call-update) | async-done | bytes 2097168 | tf_op jit(solution)/shard_map/all_gather | solution.py:82
  224.6 112.8 %while.118 = (s32[]{:T(128)}, f32[128,1024]{1,0:T(8,128)S(1)}, s32[]{:T(128)}, f32[64,8,1024]{2,1,0:T(8,128)}, f32[128]{0:T(128)S(1)}, /*index=5*/f32[512,1024]{...) while((s32[]{:T(128)}, f32[128,1024]{1,0:T(8,128)S(1)}, ...), condition=%wide.region_23.24_spmd, body=%wide.region_18.23_spmd.sunk | while | flops 9568278 | bytes 15501354 | solution.py:106
  225.9 5.5 %add_divide_fusion.7 = f32[16,128,1024]{2,1,0:T(8,128)} fusion(f32[128]{0:T(128)S(1)} %get-tuple-element.1319, f32[16,1024]{1,0:T(8,128)S(1)} %bitcast.131), kind=kLoop, calls=%fused_computation.30.clone.1 | loop fusion | flops 8388608 | bytes 8454656 | tf_op jit(solution)/shard_map/while/body/div | solution.py:24
  232.8 28.4 %while.123 = (s32[]{:T(128)}, f32[128,1024]{1,0:T(8,128)S(1)}, f32[16,128,1024]{2,1,0:T(8,128)}, f32[16,3,1024]{2,1,0:T(4,128)S(1)}, s32[]{:T(128)}, /*index=5*/s32[]{:T(128)}, s32[]{:T(128)}, s32[]{}, s32[]{}) while((s32[]{:T(128)}, f32[128,1024]{1,0:T(8,128)S(1)}, f32[16,128,1024]{2,1,0:T(8,128)}, f32[16,3,1024]{2,1,0:T(4,128)S(1)}, ...), condition=%wide.region_22.22_spmd, body=%wide.region_21.21_spmd.sunk | while | flops 917509 | bytes 4752529 | solution.py:43
  263.5 5.5 %add_divide_fusion.7 = f32[16,128,1024]{2,1,0:T(8,128)} fusion(f32[128]{0:T(128)S(1)} %get-tuple-element.1319, f32[16,1024]{1,0:T(8,128)S(1)} %bitcast.131), kind=kLoop, calls=%fused_computation.30.clone.1 | loop fusion | flops 8388608 | bytes 8454656 | tf_op jit(solution)/shard_map/while/body/div | solution.py:24
  270.4 28.3 %while.123 = (s32[]{:T(128)}, f32[128,1024]{1,0:T(8,128)S(1)}, f32[16,128,1024]{2,1,0:T(8,128)}, f32[16,3,1024]{2,1,0:T(4,128)S(1)}, s32[]{:T(128)}, /*index=5*/s32[]{:T(128)}, s32[]{:T(128)}, s32[]{}, s32[]{}) while((s32[]{:T(128)}, f32[128,1024]{1,0:T(8,128)S(1)}, f32[16,128,1024]{2,1,0:T(8,128)}, f32[16,3,1024]{2,1,0:T(4,128)S(1)}, ...), condition=%wide.region_22.22_spmd, body=%wide.region_21.21_spmd.sunk | while | flops 917509 | bytes 4752529 | solution.py:43
  301.0 5.5 %add_divide_fusion.7 = f32[16,128,1024]{2,1,0:T(8,128)} fusion(f32[128]{0:T(128)S(1)} %get-tuple-element.1319, f32[16,1024]{1,0:T(8,128)S(1)} %bitcast.131), kind=kLoop, calls=%fused_computation.30.clone.1 | loop fusion | flops 8388608 | bytes 8454656 | tf_op jit(solution)/shard_map/while/body/div | solution.py:24
  307.9 28.3 %while.123 = (s32[]{:T(128)}, f32[128,1024]{1,0:T(8,128)S(1)}, f32[16,128,1024]{2,1,0:T(8,128)}, f32[16,3,1024]{2,1,0:T(4,128)S(1)}, s32[]{:T(128)}, /*index=5*/s32[]{:T(128)}, s32[]{:T(128)}, s32[]{}, s32[]{}) while((s32[]{:T(128)}, f32[128,1024]{1,0:T(8,128)S(1)}, f32[16,128,1024]{2,1,0:T(8,128)}, f32[16,3,1024]{2,1,0:T(4,128)S(1)}, ...), condition=%wide.region_22.22_spmd, body=%wide.region_21.21_spmd.sunk | while | flops 917509 | bytes 4752529 | solution.py:43
  337.4 4.3 broadcast.113.clone.1
  341.7 41.8 %while.119 = (s32[]{:T(128)}, f32[128,1024]{1,0:T(8,128)S(1)}, f32[16,128,1024]{2,1,0:T(8,128)}, f32[16,128,1024]{2,1,0:T(8,128)}, f32[16,3,1024]{2,1,0:T(4,128)...) while((s32[]{:T(128)}, f32[128,1024]{1,0:T(8,128)S(1)}, ...), condition=%wide.region_25.26_spmd, body=%wide.region_24.25_spmd.sunk | while | flops 1048581 | bytes 5801121 | solution.py:35
  341.9 2.4 bitcast_dynamic-update-slice_fusion.5
  344.5 2.4 bitcast_dynamic-update-slice_fusion.5
  349.7 2.4 bitcast_dynamic-update-slice_fusion.5
  357.6 2.4 bitcast_dynamic-update-slice_fusion.5
  365.4 2.4 bitcast_dynamic-update-slice_fusion.5
  375.9 2.4 bitcast_dynamic-update-slice_fusion.5
  383.6 4.3 broadcast.113.clone
  387.9 41.8 %while.116 = (s32[]{:T(128)}, f32[128,1024]{1,0:T(8,128)S(1)}, f32[16,128,1024]{2,1,0:T(8,128)}, f32[16,128,1024]{2,1,0:T(8,128)}, f32[16,3,1024]{2,1,0:T(4,128)...) while((s32[]{:T(128)}, f32[128,1024]{1,0:T(8,128)S(1)}, ...), condition=%wide.region_13.14_spmd, body=%wide.region_12.13_spmd.sunk | while | flops 1048580 | bytes 5801609 | solution.py:35
  393.3 2.4 bitcast_dynamic-update-slice_fusion.4
  398.5 2.4 bitcast_dynamic-update-slice_fusion.4
  414.2 2.4 bitcast_dynamic-update-slice_fusion.4
  427.2 2.4 bitcast_dynamic-update-slice_fusion.4
  429.7 9.3 %multiply_convert_fusion = bf16[16,128,1024]{2,1,0:T(8,128)(2,1)} fusion(f32[16,128,1024]{2,1,0:T(8,128)} %get-tuple-element.568, f32[16,128,1024]{2,1,0:T(8,128)} %get-tuple-element.571), kind=kLoop, calls=%fused_computation.71 | loop fusion | flops 4194304 | bytes 20971520 | tf_op jit(solution)/shard_map/convert_element_type | solution.py:109
  (410 shorter events, 224.3 us)
Async XLA Ops:
  6.5 14.4 %copy-start = (f32[8,128]{1,0:T(8,128)S(1)}, f32[8,128]{1,0:T(8,128)}, u32[]{:S(2)}) copy-start(f32[8,128]{1,0:T(8,128)} %param.22) | copy-start | bytes 12292
  6.5 80.4 %copy-start.6 = (f32[128]{0:T(128)S(1)}, f32[128]{0:T(128)}, u32[]{:S(2)}) copy-start(f32[128]{0:T(128)} %param.21) | copy-start | bytes 1540
  6.5 80.4 %copy-start.5 = (f32[128]{0:T(128)S(1)}, f32[128]{0:T(128)}, u32[]{:S(2)}) copy-start(f32[128]{0:T(128)} %param.23) | copy-start | bytes 1540
  6.5 78.7 %all-reduce.14.cloned.1.call-start = ((), (), s32[]{:S(2)}) async-start(), calls=%async_computation | async-start | bytes 1048576 | tf_op jit(solution)/shard_map/psum | solution.py:73
  9.8 1.5 collective-permute-start
  11.3 5.3 %collective-permute-start.1 = (f32[16,1024]{1,0:T(8,128)S(1)}, f32[16,1024]{1,0:T(8,128)S(1)}, u32[]{:S(2)}, u32[]{:S(2)}) collective-permute-start(f32[16,1024]{1,0:T(8,128)S(1)} %add.341), channel_id=1, source_target_pairs={{0,2},{1,3},{2,0},{3,1},{4,6},{5,7},{6,4},{7,5},{8,10},{9,11},{10,... | collective-permute-start | bytes 196616 | tf_op jit(solution)/shard_map/ppermute | solution.py:56
  16.6 4.3 collective-permute-start.2
  28.7 149.8 %all-gather.8.cloned.1.call-start = ((), (), s32[]{:S(2)}) async-start(), calls=%async_computation.3 | async-start | bytes 2621440 | tf_op jit(solution)/shard_map/all_gather | solution.py:84
  86.3 47.1 %copy-start.4 = (f32[16,8,1024]{2,1,0:T(8,128)}, f32[16,8,1024]{2,1,0:T(8,128)S(1)}, u32[]{:S(2)}) copy-start(f32[16,8,1024]{2,1,0:T(8,128)S(1)} %broadcast_multiply_fusion) | copy-start | bytes 1572868
  132.5 0.8 copy-start.2
  133.3 91.2 %all-gather.4.cloned.1.call-start = ((), (), s32[]{:S(2)}) async-start(), calls=%async_computation.1 | async-start | bytes 2621440 | tf_op jit(solution)/shard_map/all_gather | solution.py:82
  134.1 249.4 %all-gather.6.cloned.1.call-start = ((), (), s32[]{:S(2)}) async-start(), calls=%async_computation.2 | async-start | bytes 2621440 | tf_op jit(solution)/shard_map/all_gather | solution.py:83
  165.1 0.8 copy-start.3
  429.7 9.3 %copy-start.1 = (f32[8,128]{1,0:T(8,128)S(1)}, f32[8,128]{1,0:T(8,128)}, u32[]{:S(2)}) copy-start(f32[8,128]{1,0:T(8,128)} %param.22) | copy-start | bytes 12292
Sparse Core Ops, SparseCore 0:
  28.8 56.4 all-reduce.13
  133.4 44.9 all-gather.7
  180.0 44.4 all-gather.3
  225.9 44.4 all-gather.5
